TPU v7x, 32 devices: a whole 2x2x4 slice. The times are simulated.
32 devices in a mesh: grp: 2 (over x), seq: 16 (over z, y, core).
Axes of the slice: x: 2, y: 2, z: 4, core: 2. Of those that a mesh axis runs over, the one named last changes fastest.
Arguments:
- tokens: bfloat16 [16384, 1024], P(('grp', 'seq')), parts along dimension 0, may hold values from -6 to 6
- value_weight: bfloat16 [1024, 1024], replicated, may hold values from -0.1875 to 0.1875
- gate_weight: bfloat16 [1024, 1024], replicated, may hold values from -0.1875 to 0.1875
- out_weight: bfloat16 [1024, 1024], replicated, may hold values from -0.1875 to 0.1875
- kernel_weight: bfloat16 [1024, 16], replicated, may hold values from -0.1875 to 0.1875
- kernel_bias: float32 [16], replicated, may hold values from -4 to 4
Outputs:
- mixed: bfloat16 [16384, 1024], P(('grp', 'seq')), parts along dimension 0
There are 2 independent parts, one for each index of `grp`. A program takes and returns all parts, laid end to end along the dimension named above; an argument that names none is the same for every part. Nothing has to cross between parts.
All inputs are finite; a program needn't handle non-finite values.
Results may differ from a plain program's by a relative error of at most 0.0071.
Values may be sent and summed in bfloat16 or wider, within the bound.
A program may use at most 128 MiB of HBM per device.

v0:
```python
import functools

import jax
import jax.numpy as jnp
from jax import lax
from jax.experimental import pallas as pl
from jax.experimental.pallas import tpu as pltpu
from jax.sharding import PartitionSpec as P

MESH = pl.DeviceIdType.MESH
LANES = 128
BLOCK = 256
CHUNKS = 2


def layer_kernel(
    n,
    heads,
    tokens_hbm,
    value_hbm,
    gate_hbm,
    out_hbm,
    head_ref,
    bias_ref,
    mixed_ref,
    tokens,
    value_w,
    gate_w,
    out_w,
    outgoing,
    held,
    lag_send,
    lags,
    band,
    open_gate,
    result,
    returned,
    total,
    load_sems,
    lag_sems,
    sems,
):
    rows, model = tokens.shape
    chunks, _, wide, _ = outgoing.shape
    width = chunks * wide
    length = n * rows
    per = BLOCK // width
    blocks = n // per
    share = n // heads
    me = lax.axis_index("seq")
    mine = me // per
    distance = sorted(range(blocks), key=lambda off: (-min(off, blocks - off), off))
    order = range(blocks)

    def place(off):
        return lax.rem(mine + distance[off], blocks)

    def load(source, target, slot):
        return pltpu.make_async_copy(source, target, load_sems.at[slot])

    def value_load(off):
        columns = pl.ds(pl.multiple_of(place(off) * BLOCK, BLOCK), BLOCK)
        return load(value_hbm.at[:, columns], value_w.at[off], 3 + off)

    tokens_load = load(tokens_hbm, tokens, 0)
    gate_load = load(gate_hbm, gate_w, 1)
    out_load = load(out_hbm, out_w, 2)
    barrier = pltpu.get_barrier_semaphore()

    def loop(action):
        def run(step, carry):
            action(step)
            return carry

        lax.fori_loop(1, n, run, 0)

    loop(
        lambda step: pl.semaphore_signal(
            barrier, inc=1, device_id={"seq": lax.rem(me + step, n)}, device_id_type=MESH
        )
    )

    tokens_load.start()
    for off in order:
        value_load(off).start()

    def lag_copy(step):
        peer = lax.rem(me + step, n)
        return pltpu.make_async_remote_copy(
            src_ref=lag_send.at[peer // share],
            dst_ref=lags.at[me],
            send_sem=lag_sems.at[0, step],
            recv_sem=lag_sems.at[1, step],
            device_id={"seq": peer},
            device_id_type=MESH,
        )

    def remote(kind, source, target, chunk, step):
        peer = lax.rem(me + step, n)
        return pltpu.make_async_remote_copy(
            src_ref=source.at[chunk, peer],
            dst_ref=target.at[chunk, me],
            send_sem=sems.at[2 * kind, chunk, step],
            recv_sem=sems.at[2 * kind + 1, chunk, step],
            device_id={"seq": peer},
            device_id_type=MESH,
        )

    def value_copy(chunk, step):
        return remote(0, outgoing, held, chunk, step)

    def back_copy(chunk, step):
        return remote(1, result, returned, chunk, step)

    def send_block(off, chunk, make):
        inside = lax.rem(me, per)
        for turn in range(1 if off == blocks - 1 else 0, per):
            peer = place(off) * per + lax.rem(inside + turn, per)
            make(chunk, lax.rem(peer - me + n, n)).start()

    tokens_load.wait()
    for off in order:
        value_load(off).wait()
        block = jnp.dot(tokens[...], value_w[off], preferred_element_type=jnp.float32)
        block = block.astype(jnp.bfloat16).T.reshape(per, chunks, wide, rows)
        for chunk in range(chunks):
            outgoing[chunk, pl.ds(place(off) * per, per)] = block[:, chunk]
        if off == 0:
            pl.semaphore_wait(barrier, n - 1)
        send_block(off, 0, value_copy)
        if off == 0:
            gate_load.start()
            out_load.start()
            logits = lax.dot_general(
                head_ref[...], tokens[...], (((1,), (1,)), ((), ())), preferred_element_type=jnp.float32
            )
            for head in range(heads):
                made = jnp.tanh(logits[head : head + 1] + bias_ref[0, head]) * length ** (-0.5)
                lag_send[head] = made.astype(jnp.bfloat16).astype(jnp.float32)
            loop(lambda step: lag_copy(step).start())
            lags[me] = lag_send[me // share]
    for chunk in range(1, chunks):
        for off in order:
            send_block(off, chunk, value_copy)
    for chunk in range(chunks):
        held[chunk, me] = outgoing[chunk, me]

    loop(lambda step: lag_copy(step).wait())
    row = jnp.concatenate([lags[source] for source in range(n)], axis=1)
    row = jnp.concatenate([row[:, length - rows - LANES :], row], axis=1)
    for start in range(0, length + rows, rows):
        piece = jnp.broadcast_to(row[:, start : start + rows + LANES], (LANES, rows + LANES))
        turned = pltpu.roll(piece, 0, 1, stride=1, stride_axis=0)[:, LANES:]
        band[:, start : start + rows] = turned.astype(jnp.bfloat16)

    gate_load.wait()
    for part in range(model // BLOCK):
        gate = jnp.dot(
            tokens[...], gate_w[:, part * BLOCK : (part + 1) * BLOCK], preferred_element_type=jnp.float32
        )
        gate = (gate / (1.0 + jnp.exp(-gate))).T.reshape(per, chunks, wide, rows)
        for chunk in range(chunks):
            open_gate[chunk, part * per : (part + 1) * per] = gate[:, chunk]

    group = min(n, max(1, BLOCK // wide))
    reach = min(n, 16)

    def convolve(chunk, carry):
        loop(lambda step: value_copy(chunk, step).wait())
        held[chunk, n : 2 * n] = held[chunk, 0:n]

        def outputs(index, inner):
            first = index * group
            summed = None
            for base in range(0, n, reach):
                left = jnp.concatenate(
                    [
                        held[chunk, pl.ds(first + at, group)].reshape(group * wide, rows)
                        for at in range(base, base + reach)
                    ],
                    axis=1,
                )
                right = jnp.concatenate(
                    [
                        band[:, pl.ds((rows - at) if at <= rows else length + rows - at, rows)]
                        for at in range(base * rows, (base + reach) * rows, LANES)
                    ],
                    axis=0,
                )
                term = jnp.dot(left, right, preferred_element_type=jnp.float32)
                summed = term if summed is None else summed + term
            result[chunk, pl.ds(first, group)] = summed.astype(jnp.bfloat16).reshape(group, wide, rows)
            return inner

        lax.fori_loop(0, n // group, outputs, 0)
        for off in order:
            send_block(off, chunk, back_copy)
        returned[chunk, me] = result[chunk, me]
        return carry

    lax.fori_loop(0, chunks, convolve, 0)

    out_load.wait()
    part = n // 2
    for chunk in range(chunks):
        for far in range(2):
            base = (me // part) * part if far == 0 else (1 - me // part) * part

            def arrive(index, carry):
                step = lax.rem(me - (base + index) + n, n)

                @pl.when(step > 0)
                def _():
                    back_copy(chunk, step).wait_recv()

                return carry

            lax.fori_loop(0, part, arrive, 0)
            chosen = pl.ds(base, part)
            gated = returned[chunk, chosen].astype(jnp.float32) * open_gate[chunk, chosen]
            gated = gated.astype(jnp.bfloat16).reshape(part * wide, rows).T
            weight = out_w[chosen, chunk].reshape(part * wide, model)
            term = jnp.dot(gated, weight, preferred_element_type=jnp.float32)
            if chunk + far > 0:
                term = total[...] + term
            if chunk + far < chunks:
                total[...] = term
            else:
                mixed_ref[...] = term.astype(jnp.bfloat16)
    for chunk in range(chunks):
        loop(lambda step: back_copy(chunk, step).wait_send())


def body(tokens, value_weight, gate_weight, out_weight, kernel_weight, kernel_bias):
    rows, model = tokens.shape
    heads = kernel_weight.shape[1]
    n = lax.axis_size("seq")
    width = model // n
    chunks = max(1, min(CHUNKS, width // 16))
    wide = width // chunks
    length = rows * n
    per = BLOCK // width
    vmem = pl.BlockSpec(memory_space=pltpu.VMEM)
    anywhere = pl.BlockSpec(memory_space=pl.ANY)
    half = jnp.bfloat16
    return pl.pallas_call(
        functools.partial(layer_kernel, n, heads),
        out_shape=jax.ShapeDtypeStruct((rows, model), half),
        in_specs=[anywhere] * 4 + [vmem, pl.BlockSpec(memory_space=pltpu.SMEM)],
        out_specs=vmem,
        scratch_shapes=[
            pltpu.VMEM((rows, model), half),
            pltpu.VMEM((n // per, model, BLOCK), half),
            pltpu.VMEM((model, model), half),
            pltpu.VMEM((n, chunks, wide, model), half),
            pltpu.VMEM((chunks, n, wide, rows), half),
            pltpu.VMEM((chunks, 2 * n, wide, rows), half),
            pltpu.VMEM((heads, 1, rows), jnp.float32),
            pltpu.VMEM((n, 1, rows), jnp.float32),
            pltpu.VMEM((LANES, length + rows), half),
            pltpu.VMEM((chunks, n, wide, rows), jnp.float32),
            pltpu.VMEM((chunks, n, wide, rows), half),
            pltpu.VMEM((chunks, n, wide, rows), half),
            pltpu.VMEM((rows, model), jnp.float32),
            pltpu.SemaphoreType.DMA((3 + n // per,)),
            pltpu.SemaphoreType.DMA((2, n)),
            pltpu.SemaphoreType.DMA((4, chunks, n)),
        ],
        compiler_params=pltpu.CompilerParams(
            collective_id=0, has_side_effects=True, vmem_limit_bytes=60 * 2**20
        ),
    )(
        tokens,
        value_weight,
        gate_weight,
        out_weight.reshape(n, chunks, wide, model),
        kernel_weight.T,
        kernel_bias.reshape(1, heads),
    )


def solution(mesh):
    placed = (P(("grp", "seq"), None), P(), P(), P(), P(), P())
    return jax.shard_map(
        body, mesh=mesh, in_specs=placed, out_specs=P(("grp", "seq"), None), check_vma=False
    )
```

profile of v0, /device:TPU:9, one launch (start us, length us, event | category | flops | bytes accessed | tf_op | source)
XLA Modules:
  0.0 57.3 jit_solution(11346385593129777345)
XLA Ops:
  0.0 55.0 %shard_map.64 = bf16[512,1024]{1,0:T(8,128)(2,1)} custom-call(bf16[512,1024]{1,0:T(8,128)(2,1)} %tokens_hbm.1, bf16[1024,1024]{1,0:T(8,128)(2,1)} %value_hbm.1, bf16[1024,1024]{1,0:T(8,128)(2,1)} %gate_hbm.1, bf16[16,2,32,1024]{3,2,1,0:T(8,128)(2,1)} %bitcast.3, bf16[16,1024]{1,0:T(8,128)(2,1)} %bitcast.4, f32[1,16]{1,0:T(1,128)} %bitcast.5), custom_call_target="tpu_custom_call" | custom-call | tf_op jit(solution)/shard_map/pallas_call | solution.py:246
  55.1 2.3 %copy.8 = bf16[512,1024]{1,0:T(8,128)(2,1)} copy(bf16[512,1024]{1,0:T(8,128)(2,1)} %shard_map.64) | data formatting | bytes 2097152
where the time goes:
time: 57.5 us; the launch traced here: 57.3 us
  Pallas kernels  55 us (96%)
  local copies, waits for them, and re-layouts  2.26 us (4%)
    pallas_call x1, Pallas kernels, body(): pl.pallas_call(functools.partial(layer_kernel, n, heads), out_shape=jax.S...  55 us
    unnamed x1, local copies, waits for them, and re-layouts  2.26 us

commit v1 on v0

v1 whole, which is shorter than its diff:
```python
import functools

import jax
import jax.numpy as jnp
from jax import lax
from jax.experimental import pallas as pl
from jax.experimental.pallas import tpu as pltpu
from jax.sharding import PartitionSpec as P

MESH = pl.DeviceIdType.MESH
LANES = 128
BLOCK = 256
CHUNKS = 2


def layer_kernel(
    n,
    tokens_hbm,
    value_hbm,
    gate_hbm,
    out_hbm,
    head_hbm,
    bias_hbm,
    mixed_ref,
    tokens,
    value_w,
    gate_w,
    out_w,
    head_w,
    bias,
    outgoing,
    held,
    lag_send,
    lags,
    band,
    open_gate,
    result,
    returned,
    total,
    load_sems,
    entry_sems,
    lag_sems,
    sems,
):
    rows, model = tokens.shape
    heads = head_w.shape[0]
    chunks, _, wide, _ = outgoing.shape
    width = chunks * wide
    length = n * rows
    per = BLOCK // width
    blocks = n // per
    half = blocks // 2
    bits = per.bit_length() - 1
    share = n // heads
    me = lax.axis_index("seq")
    mine = me // per
    inside = lax.rem(me, per)
    lower = mine < half
    depth = jnp.where(lower, mine, blocks - 1 - mine)
    inward = jnp.where(lower, me + per, me - per)
    outward = jnp.where(lower, me - per, me + per)
    innermost = depth == half - 1
    outermost = depth == 0

    def place(off):
        ahead = half + off if off < half else lax.rem(depth + 1 + off - half, half)
        return jnp.where(lower, ahead, blocks - 1 - ahead)

    def load(source, target, slot):
        return pltpu.make_async_copy(source, target, load_sems.at[slot])

    def value_load(off):
        columns = pl.ds(pl.multiple_of(place(off) * BLOCK, BLOCK), BLOCK)
        return load(value_hbm.at[:, columns], value_w.at[off], 5 + off)

    tokens_load = load(tokens_hbm, tokens, 0)
    gate_load = load(gate_hbm, gate_w, 1)
    out_load = load(out_hbm, out_w, 2)
    head_load = load(head_hbm, head_w, 3)
    bias_load = load(bias_hbm, bias, 4)
    barrier = pltpu.get_barrier_semaphore()

    def signal(semaphore, peer):
        pl.semaphore_signal(semaphore, inc=1, device_id={"seq": peer}, device_id_type=MESH)

    def loop(action):
        def run(step, carry):
            action(step)
            return carry

        lax.fori_loop(1, n, run, 0)

    @pl.when(innermost)
    def _():
        signal(barrier, inward)

    for bit in range(bits):
        signal(barrier, me ^ (1 << bit))

    @pl.when(jnp.logical_not(outermost))
    def _():
        signal(barrier, outward)

    tokens_load.start()
    value_load(0).start()

    def lag_copy(step):
        peer = lax.rem(me + step, n)
        return pltpu.make_async_remote_copy(
            src_ref=lag_send.at[peer // share],
            dst_ref=lags.at[me],
            send_sem=lag_sems.at[0, step],
            recv_sem=lag_sems.at[1, step],
            device_id={"seq": peer},
            device_id_type=MESH,
        )

    def remote(kind, source, target, chunk, step):
        peer = lax.rem(me + step, n)
        return pltpu.make_async_remote_copy(
            src_ref=source.at[chunk, peer],
            dst_ref=target.at[chunk, me],
            send_sem=sems.at[2 * kind, chunk, step],
            recv_sem=sems.at[2 * kind + 1, chunk, step],
            device_id={"seq": peer},
            device_id_type=MESH,
        )

    def value_copy(chunk, step):
        return remote(0, outgoing, held, chunk, step)

    def back_copy(chunk, step):
        return remote(1, result, returned, chunk, step)

    def send_block(off, chunk, make, first=0, last=per):
        for turn in range(max(first, 1) if off == blocks - 1 else first, last):
            peer = place(off) * per + lax.rem(inside + turn, per)
            make(chunk, lax.rem(peer - me + n, n)).start()

    def project(off):
        value_load(off).wait()
        block = jnp.dot(tokens[...], value_w[off], preferred_element_type=jnp.float32)
        block = block.astype(jnp.bfloat16).T.reshape(per, chunks, wide, rows)
        for chunk in range(chunks):
            outgoing[chunk, pl.ds(place(off) * per, per)] = block[:, chunk]

    def swap(bit):
        signal(entry_sems.at[bit], me ^ (1 << bit))

    def swapped(bit):
        pl.semaphore_wait(entry_sems.at[bit], 1)

    def gather():
        @pl.when(jnp.logical_not(outermost))
        def _():
            pl.semaphore_wait(entry_sems.at[bits], 1)

        @pl.when(innermost)
        def _():
            signal(entry_sems.at[bits + 1], inward)

        @pl.when(jnp.logical_not(innermost | outermost))
        def _():
            signal(entry_sems.at[bits], inward)

    def spread():
        pl.semaphore_wait(entry_sems.at[bits + 1], 1)

        @pl.when(jnp.logical_not(outermost))
        def _():
            signal(entry_sems.at[bits + 1], outward)

    pl.semaphore_wait(barrier, bits + 1)
    for bit in range(min(bits, 1)):
        swap(bit)
    tokens_load.wait()
    project(0)
    for off in range(1, blocks):
        value_load(off).start()
    head_load.start()
    bias_load.start()

    @pl.when(innermost)
    def _():
        send_block(0, 0, value_copy, 0, 1)

    for bit in range(bits):
        if bit > 0:
            swap(bit)
        swapped(bit)

    @pl.when(outermost & jnp.logical_not(innermost))
    def _():
        signal(entry_sems.at[bits], inward)

    @pl.when(innermost)
    def _():
        send_block(0, 0, value_copy, 1, per)

    known = min(2, blocks - 1)
    for off in range(1, blocks):
        project(off)
        if off == 1:
            gate_load.start()
            out_load.start()
            gather()
        if off == known:
            head_load.wait()
            bias_load.wait()
            logits = lax.dot_general(
                head_w[...], tokens[...], (((1,), (1,)), ((), ())), preferred_element_type=jnp.float32
            )
            across = lax.broadcasted_iota(jnp.int32, (heads, heads), 1)
            down = lax.broadcasted_iota(jnp.int32, (heads, heads), 0)
            column = jnp.where(across == down, jnp.broadcast_to(bias[...], (heads, heads)), 0.0)
            column = jnp.sum(column, axis=1, keepdims=True)
            made = jnp.tanh(logits + column) * length ** (-0.5)
            for head in range(heads):
                pieces = [
                    made[head : head + 1, start : start + LANES] for start in range(0, rows, LANES)
                ]
                lag_send[head] = jnp.concatenate(pieces, axis=0).astype(jnp.bfloat16)
            spread()

            @pl.when(jnp.logical_not(innermost))
            def _():
                send_block(0, 0, value_copy)

            for earlier in range(1, off + 1):
                send_block(earlier, 0, value_copy)
            loop(lambda step: lag_copy(step).start())
            lags[me] = lag_send[me // share]
        elif off > known:
            send_block(off, 0, value_copy)
    for chunk in range(1, chunks):
        for off in range(blocks):
            send_block(off, chunk, value_copy)
    for chunk in range(chunks):
        held[chunk, me] = outgoing[chunk, me]

    gate_load.wait()
    for part in range(model // BLOCK):
        gate = jnp.dot(
            tokens[...], gate_w[:, part * BLOCK : (part + 1) * BLOCK], preferred_element_type=jnp.float32
        )
        gate = (gate / (1.0 + jnp.exp(-gate))).T.reshape(per, chunks, wide, rows)
        for chunk in range(chunks):
            open_gate[chunk, part * per : (part + 1) * per] = gate[:, chunk]

    loop(lambda step: lag_copy(step).wait())
    pieces = []
    for source in range(n):
        lag = lags[source].astype(jnp.float32)
        pieces += [lag[index : index + 1] for index in range(rows // LANES)]
    row = jnp.concatenate(pieces[-(rows // LANES) - 1 :] + pieces, axis=1)
    for start in range(0, length + rows, rows):
        piece = jnp.broadcast_to(row[:, start : start + rows + LANES], (LANES, rows + LANES))
        turned = pltpu.roll(piece, 0, 1, stride=1, stride_axis=0)[:, LANES:]
        band[:, start : start + rows] = turned.astype(jnp.bfloat16)

    part = n // 2
    group = min(part, max(1, BLOCK // wide))
    reach = min(n, 16)

    def convolve(chunk, carry):
        loop(lambda step: value_copy(chunk, step).wait())
        held[chunk, n : 2 * n] = held[chunk, 0:n]
        for far in range(2):
            base = jnp.where(lower == (far == 0), part, 0)

            def outputs(index, inner):
                first = base + index * group
                summed = None
                for start in range(0, n, reach):
                    left = jnp.concatenate(
                        [
                            held[chunk, pl.ds(first + at, group)].reshape(group * wide, rows)
                            for at in range(start, start + reach)
                        ],
                        axis=1,
                    )
                    right = jnp.concatenate(
                        [
                            band[:, pl.ds((rows - at) if at <= rows else length + rows - at, rows)]
                            for at in range(start * rows, (start + reach) * rows, LANES)
                        ],
                        axis=0,
                    )
                    term = jnp.dot(left, right, preferred_element_type=jnp.float32)
                    summed = term if summed is None else summed + term
                result[chunk, pl.ds(first, group)] = summed.astype(jnp.bfloat16).reshape(group, wide, rows)
                return inner

            lax.fori_loop(0, part // group, outputs, 0)
            for off in reversed(range(half)) if far == 0 else range(half, blocks):
                send_block(off, chunk, back_copy)
        returned[chunk, me] = result[chunk, me]
        return carry

    lax.fori_loop(0, chunks, convolve, 0)

    out_load.wait()
    for chunk in range(chunks):
        for far in range(2):
            base = jnp.where(lower == (far == 0), 0, part)

            def arrive(index, carry):
                step = lax.rem(me - (base + index) + n, n)

                @pl.when(step > 0)
                def _():
                    back_copy(chunk, step).wait_recv()

                return carry

            lax.fori_loop(0, part, arrive, 0)
            chosen = pl.ds(base, part)
            gated = returned[chunk, chosen].astype(jnp.float32) * open_gate[chunk, chosen]
            gated = gated.astype(jnp.bfloat16).reshape(part * wide, rows).T
            weight = out_w[chosen, chunk].reshape(part * wide, model)
            term = jnp.dot(gated, weight, preferred_element_type=jnp.float32)
            if chunk + far > 0:
                term = total[...] + term
            if chunk + far < chunks:
                total[...] = term
            else:
                mixed_ref[...] = term.astype(jnp.bfloat16)
    for chunk in range(chunks):
        loop(lambda step: back_copy(chunk, step).wait_send())


def body(tokens, value_weight, gate_weight, out_weight, kernel_weight, kernel_bias):
    rows, model = tokens.shape
    heads = kernel_weight.shape[1]
    n = lax.axis_size("seq")
    width = model // n
    chunks = max(1, min(CHUNKS, width // 16))
    wide = width // chunks
    length = rows * n
    per = BLOCK // width
    half = jnp.bfloat16
    operands = (
        tokens,
        value_weight,
        gate_weight,
        out_weight.reshape(n, chunks, wide, model),
        kernel_weight.T,
        kernel_bias.reshape(1, heads),
    )
    return pl.pallas_call(
        functools.partial(layer_kernel, n),
        out_shape=pltpu.VMEM((rows, model), half),
        in_specs=[pl.BlockSpec(memory_space=pl.ANY)] * len(operands),
        out_specs=pl.BlockSpec(memory_space=pltpu.VMEM),
        scratch_shapes=[
            pltpu.VMEM((rows, model), half),
            pltpu.VMEM((n // per, model, BLOCK), half),
            pltpu.VMEM((model, model), half),
            pltpu.VMEM((n, chunks, wide, model), half),
            pltpu.VMEM((heads, model), half),
            pltpu.VMEM((1, heads), jnp.float32),
            pltpu.VMEM((chunks, n, wide, rows), half),
            pltpu.VMEM((chunks, 2 * n, wide, rows), half),
            pltpu.VMEM((heads, rows // LANES, LANES), half),
            pltpu.VMEM((n, rows // LANES, LANES), half),
            pltpu.VMEM((LANES, length + rows), half),
            pltpu.VMEM((chunks, n, wide, rows), jnp.float32),
            pltpu.VMEM((chunks, n, wide, rows), half),
            pltpu.VMEM((chunks, n, wide, rows), half),
            pltpu.VMEM((rows, model), jnp.float32),
            pltpu.SemaphoreType.DMA((5 + n // per,)),
            pltpu.SemaphoreType.REGULAR((per.bit_length() + 1,)),
            pltpu.SemaphoreType.DMA((2, n)),
            pltpu.SemaphoreType.DMA((4, chunks, n)),
        ],
        compiler_params=pltpu.CompilerParams(
            collective_id=0, has_side_effects=True, vmem_limit_bytes=48 * 2**20
        ),
    )(*[pltpu.with_memory_space_constraint(operand, pltpu.HBM) for operand in operands])


def solution(mesh):
    placed = (P(("grp", "seq"), None), P(), P(), P(), P(), P())
    return jax.shard_map(
        body, mesh=mesh, in_specs=placed, out_specs=P(("grp", "seq"), None), check_vma=False
    )
```

time: 57.5 us -> 54.4 us (0.946)
  Pallas kernels: 55 us -> 53.1 us
  local copies, waits for them, and re-layouts: 2.26 us -> 0.97 us
    pallas_call x1, Pallas kernels: 55 us -> 53.1 us  [body(): pl.pallas_call(functools.partial(layer_kernel, n), out_shape=pltpu.VMEM((...]
    unnamed x1, local copies, waits for them, and re-layouts: 2.26 us -> 0.97 us
where the time goes in v1:
time: 54.4 us; the launch traced here: 54.1 us
  Pallas kernels  53.1 us (98%)
  local copies, waits for them, and re-layouts  0.97 us (2%)
    pallas_call x1, Pallas kernels, body(): pl.pallas_call(functools.partial(layer_kernel, n), out_shape=pltpu.VMEM((...  53.1 us

profile of v1, /device:TPU:9, one launch (start us, length us, event | category | flops | bytes accessed | tf_op | source)
XLA Modules:
  0.0 54.1 jit_solution(8981357596853719641)
XLA Ops:
  0.0 53.1 %shard_map.64 = bf16[512,1024]{1,0:T(8,128)(2,1)S(1)} custom-call(bf16[512,1024]{1,0:T(8,128)(2,1)} %tokens_hbm.1, bf16[1024,1024]{1,0:T(8,128)(2,1)} %value_hbm.1, bf16[1024,1024]{1,0:T(8,128)(2,1)} %gate_hbm.1, bf16[16,2,32,1024]{3,2,1,0:T(8,128)(2,1)} %bitcast.3, bf16[16,1024]{1,0:T(8,128)(2,1)} %bitcast.4, f32[1,16]{1,0:T(1,128)} %bitcast.5), custom_call_target="tpu_custom_call" | custom-call | tf_op jit(solution)/shard_map/pallas_call | solution.py:350
  53.1 1.0 %copy.8 = bf16[512,1024]{1,0:T(8,128)(2,1)} copy(bf16[512,1024]{1,0:T(8,128)(2,1)S(1)} %shard_map.64) | data formatting | bytes 2097152

commit v2 on v1

--- a/solution.py
+++ b/solution.py
@@ -109,28 +109,32 @@
         return pltpu.make_async_remote_copy(
             src_ref=lag_send.at[peer // share],
             dst_ref=lags.at[me],
-            send_sem=lag_sems.at[0, step],
-            recv_sem=lag_sems.at[1, step],
+            send_sem=lag_sems.at[0],
+            recv_sem=lag_sems.at[1],
             device_id={"seq": peer},
             device_id_type=MESH,
         )
 
-    def remote(kind, source, target, chunk, step):
+    def remote(source, target, chunk, step, sent, received):
         peer = lax.rem(me + step, n)
         return pltpu.make_async_remote_copy(
             src_ref=source.at[chunk, peer],
             dst_ref=target.at[chunk, me],
-            send_sem=sems.at[2 * kind, chunk, step],
-            recv_sem=sems.at[2 * kind + 1, chunk, step],
+            send_sem=sems.at[sent],
+            recv_sem=sems.at[received],
             device_id={"seq": peer},
             device_id_type=MESH,
         )
 
     def value_copy(chunk, step):
-        return remote(0, outgoing, held, chunk, step)
+        return remote(outgoing, held, chunk, step, 0, 2 + chunk)
 
     def back_copy(chunk, step):
-        return remote(1, result, returned, chunk, step)
+        near = (lax.rem(me + step, n) < half * per) == lower
+        return remote(result, returned, chunk, step, 1, 2 + chunks + 2 * chunk + jnp.where(near, 0, 1))
+
+    def finish(slots, semaphore):
+        pltpu.make_async_copy(slots, slots, semaphore).wait()
 
     def send_block(off, chunk, make, first=0, last=per):
         for turn in range(max(first, 1) if off == blocks - 1 else first, last):
@@ -182,7 +186,8 @@
 
     @pl.when(innermost)
     def _():
-        send_block(0, 0, value_copy, 0, 1)
+        for chunk in range(chunks):
+            send_block(0, chunk, value_copy, 0, 1)
 
     for bit in range(bits):
         if bit > 0:
@@ -233,7 +238,9 @@
         elif off > known:
             send_block(off, 0, value_copy)
     for chunk in range(1, chunks):
-        for off in range(blocks):
+        pl.when(jnp.logical_not(innermost))(functools.partial(send_block, 0, chunk, value_copy, 0, 1))
+        send_block(0, chunk, value_copy, 1, per)
+        for off in range(1, blocks):
             send_block(off, chunk, value_copy)
     for chunk in range(chunks):
         held[chunk, me] = outgoing[chunk, me]
@@ -247,7 +254,7 @@
         for chunk in range(chunks):
             open_gate[chunk, part * per : (part + 1) * per] = gate[:, chunk]
 
-    loop(lambda step: lag_copy(step).wait())
+    finish(lags.at[pl.ds(0, n - 1)], lag_sems.at[1])
     pieces = []
     for source in range(n):
         lag = lags[source].astype(jnp.float32)
@@ -263,7 +270,7 @@
     reach = min(n, 16)
 
     def convolve(chunk, carry):
-        loop(lambda step: value_copy(chunk, step).wait())
+        finish(held.at[chunk, pl.ds(0, n - 1)], sems.at[2 + chunk])
         held[chunk, n : 2 * n] = held[chunk, 0:n]
         for far in range(2):
             base = jnp.where(lower == (far == 0), part, 0)
@@ -304,16 +311,7 @@
         for far in range(2):
             base = jnp.where(lower == (far == 0), 0, part)
 
-            def arrive(index, carry):
-                step = lax.rem(me - (base + index) + n, n)
-
-                @pl.when(step > 0)
-                def _():
-                    back_copy(chunk, step).wait_recv()
-
-                return carry
-
-            lax.fori_loop(0, part, arrive, 0)
+            finish(returned.at[chunk, pl.ds(0, part - 1 + far)], sems.at[2 + chunks + 2 * chunk + far])
             chosen = pl.ds(base, part)
             gated = returned[chunk, chosen].astype(jnp.float32) * open_gate[chunk, chosen]
             gated = gated.astype(jnp.bfloat16).reshape(part * wide, rows).T
@@ -325,8 +323,9 @@
                 total[...] = term
             else:
                 mixed_ref[...] = term.astype(jnp.bfloat16)
-    for chunk in range(chunks):
-        loop(lambda step: back_copy(chunk, step).wait_send())
+    finish(lags.at[pl.ds(0, n - 1)], lag_sems.at[0])
+    for sent in range(2):
+        finish(returned.at[:, pl.ds(0, n - 1)], sems.at[sent])
 
 
 def body(tokens, value_weight, gate_weight, out_weight, kernel_weight, kernel_bias):
@@ -370,8 +369,8 @@
             pltpu.VMEM((rows, model), jnp.float32),
             pltpu.SemaphoreType.DMA((5 + n // per,)),
             pltpu.SemaphoreType.REGULAR((per.bit_length() + 1,)),
-            pltpu.SemaphoreType.DMA((2, n)),
-            pltpu.SemaphoreType.DMA((4, chunks, n)),
+            pltpu.SemaphoreType.DMA((2,)),
+            pltpu.SemaphoreType.DMA((2 + 3 * chunks,)),
         ],
         compiler_params=pltpu.CompilerParams(
             collective_id=0, has_side_effects=True, vmem_limit_bytes=48 * 2**20

time: 54.4 us -> 52.4 us (0.963)
  Pallas kernels: 53.1 us -> 51.3 us
    pallas_call x1, Pallas kernels: 53.1 us -> 51.3 us  [body(): pl.pallas_call(functools.partial(layer_kernel, n), out_shape=pltpu.VMEM((...]
where the time goes in v2:
time: 52.4 us; the launch traced here: 52.3 us
  Pallas kernels  51.3 us (98%)
  local copies, waits for them, and re-layouts  0.97 us (2%)
    pallas_call x1, Pallas kernels, body(): pl.pallas_call(functools.partial(layer_kernel, n), out_shape=pltpu.VMEM((...  51.3 us

profile of v2, /device:TPU:9, one launch (start us, length us, event | category | flops | bytes accessed | tf_op | source)
XLA Modules:
  0.0 52.3 jit_solution(15966873711357891503)
XLA Ops:
  0.0 51.3 %shard_map.64 = bf16[512,1024]{1,0:T(8,128)(2,1)S(1)} custom-call(bf16[512,1024]{1,0:T(8,128)(2,1)} %tokens_hbm.1, bf16[1024,1024]{1,0:T(8,128)(2,1)} %value_hbm.1, bf16[1024,1024]{1,0:T(8,128)(2,1)} %gate_hbm.1, bf16[16,2,32,1024]{3,2,1,0:T(8,128)(2,1)} %bitcast.3, bf16[16,1024]{1,0:T(8,128)(2,1)} %bitcast.4, f32[1,16]{1,0:T(1,128)} %bitcast.5), custom_call_target="tpu_custom_call" | custom-call | tf_op jit(solution)/shard_map/pallas_call | solution.py:349
  51.3 1.0 %copy.8 = bf16[512,1024]{1,0:T(8,128)(2,1)} copy(bf16[512,1024]{1,0:T(8,128)(2,1)S(1)} %shard_map.64) | data formatting | bytes 2097152

commit v3 on v2

--- a/solution.py
+++ b/solution.py
@@ -202,14 +202,22 @@
     def _():
         send_block(0, 0, value_copy, 1, per)
 
-    known = min(2, blocks - 1)
+    gather()
+    known = min(1, blocks - 1)
     for off in range(1, blocks):
         project(off)
         if off == 1:
             gate_load.start()
             out_load.start()
-            gather()
         if off == known:
+            spread()
+
+            @pl.when(jnp.logical_not(innermost))
+            def _():
+                send_block(0, 0, value_copy)
+
+            for earlier in range(1, off + 1):
+                send_block(earlier, 0, value_copy)
             head_load.wait()
             bias_load.wait()
             logits = lax.dot_general(
@@ -225,14 +233,6 @@
                     made[head : head + 1, start : start + LANES] for start in range(0, rows, LANES)
                 ]
                 lag_send[head] = jnp.concatenate(pieces, axis=0).astype(jnp.bfloat16)
-            spread()
-
-            @pl.when(jnp.logical_not(innermost))
-            def _():
-                send_block(0, 0, value_copy)
-
-            for earlier in range(1, off + 1):
-                send_block(earlier, 0, value_copy)
             loop(lambda step: lag_copy(step).start())
             lags[me] = lag_send[me // share]
         elif off > known:

time: 52.4 us -> 52.4 us (level)
  no operation moved by 1% of the time
where the time goes in v3:
time: 52.4 us; the launch traced here: 52.3 us
  Pallas kernels  51.3 us (98%)
  local copies, waits for them, and re-layouts  0.97 us (2%)
    pallas_call x1, Pallas kernels, body(): pl.pallas_call(functools.partial(layer_kernel, n), out_shape=pltpu.VMEM((...  51.3 us

profile of v3, /device:TPU:9, one launch (start us, length us, event | category | flops | bytes accessed | tf_op | source)
XLA Modules:
  0.0 52.3 jit_solution(7919884584358702942)
XLA Ops:
  0.0 51.3 %shard_map.64 = bf16[512,1024]{1,0:T(8,128)(2,1)S(1)} custom-call(bf16[512,1024]{1,0:T(8,128)(2,1)} %tokens_hbm.1, bf16[1024,1024]{1,0:T(8,128)(2,1)} %value_hbm.1, bf16[1024,1024]{1,0:T(8,128)(2,1)} %gate_hbm.1, bf16[16,2,32,1024]{3,2,1,0:T(8,128)(2,1)} %bitcast.3, bf16[16,1024]{1,0:T(8,128)(2,1)} %bitcast.4, f32[1,16]{1,0:T(1,128)} %bitcast.5), custom_call_target="tpu_custom_call" | custom-call | tf_op jit(solution)/shard_map/pallas_call | solution.py:349
  51.3 1.0 %copy.8 = bf16[512,1024]{1,0:T(8,128)(2,1)} copy(bf16[512,1024]{1,0:T(8,128)(2,1)S(1)} %shard_map.64) | data formatting | bytes 2097152

commit v4 on v3

--- a/solution.py
+++ b/solution.py
@@ -71,13 +71,23 @@
 
     def value_load(off):
         columns = pl.ds(pl.multiple_of(place(off) * BLOCK, BLOCK), BLOCK)
-        return load(value_hbm.at[:, columns], value_w.at[off], 5 + off)
-
-    tokens_load = load(tokens_hbm, tokens, 0)
-    gate_load = load(gate_hbm, gate_w, 1)
-    out_load = load(out_hbm, out_w, 2)
-    head_load = load(head_hbm, head_w, 3)
-    bias_load = load(bias_hbm, bias, 4)
+        return load(value_hbm.at[:, columns], value_w.at[off], 3 + off)
+
+    middle = model // 2
+    first_loads = []
+    for index in range(2):
+        deep = pl.ds(index * middle, middle)
+        columns = pl.ds(pl.multiple_of(place(0) * BLOCK, BLOCK), BLOCK)
+        first_loads.append(
+            (
+                load(tokens_hbm.at[:, deep], tokens.at[:, deep], 4 + blocks + 2 * index),
+                load(value_hbm.at[deep, columns], value_w.at[0, deep], 5 + blocks + 2 * index),
+            )
+        )
+    gate_load = load(gate_hbm, gate_w, 0)
+    out_load = load(out_hbm, out_w, 1)
+    head_load = load(head_hbm, head_w, 2)
+    bias_load = load(bias_hbm, bias, 3)
     barrier = pltpu.get_barrier_semaphore()
 
     def signal(semaphore, peer):
@@ -101,8 +111,9 @@
     def _():
         signal(barrier, outward)
 
-    tokens_load.start()
-    value_load(0).start()
+    for pair in first_loads:
+        for part in pair:
+            part.start()
 
     def lag_copy(step):
         peer = lax.rem(me + step, n)
@@ -142,8 +153,17 @@
             make(chunk, lax.rem(peer - me + n, n)).start()
 
     def project(off):
-        value_load(off).wait()
-        block = jnp.dot(tokens[...], value_w[off], preferred_element_type=jnp.float32)
+        if off > 0:
+            value_load(off).wait()
+            block = jnp.dot(tokens[...], value_w[off], preferred_element_type=jnp.float32)
+        else:
+            block = None
+            for index, pair in enumerate(first_loads):
+                for part in pair:
+                    part.wait()
+                deep = slice(index * middle, (index + 1) * middle)
+                term = jnp.dot(tokens[:, deep], value_w[0, deep], preferred_element_type=jnp.float32)
+                block = term if block is None else block + term
         block = block.astype(jnp.bfloat16).T.reshape(per, chunks, wide, rows)
         for chunk in range(chunks):
             outgoing[chunk, pl.ds(place(off) * per, per)] = block[:, chunk]
@@ -177,7 +197,6 @@
     pl.semaphore_wait(barrier, bits + 1)
     for bit in range(min(bits, 1)):
         swap(bit)
-    tokens_load.wait()
     project(0)
     for off in range(1, blocks):
         value_load(off).start()
@@ -367,7 +386,7 @@
             pltpu.VMEM((chunks, n, wide, rows), half),
             pltpu.VMEM((chunks, n, wide, rows), half),
             pltpu.VMEM((rows, model), jnp.float32),
-            pltpu.SemaphoreType.DMA((5 + n // per,)),
+            pltpu.SemaphoreType.DMA((8 + n // per,)),
             pltpu.SemaphoreType.REGULAR((per.bit_length() + 1,)),
             pltpu.SemaphoreType.DMA((2,)),
             pltpu.SemaphoreType.DMA((2 + 3 * chunks,)),

time: 52.4 us -> 52.4 us (level)
  no operation moved by 1% of the time
where the time goes in v4:
time: 52.4 us; the launch traced here: 52.3 us
  Pallas kernels  51.3 us (98%)
  local copies, waits for them, and re-layouts  0.97 us (2%)
    pallas_call x1, Pallas kernels, body(): pl.pallas_call(functools.partial(layer_kernel, n), out_shape=pltpu.VMEM((...  51.3 us

profile of v4, /device:TPU:9, one launch (start us, length us, event | category | flops | bytes accessed | tf_op | source)
XLA Modules:
  0.0 52.3 jit_solution(3014467102164461267)
XLA Ops:
  0.0 51.3 %shard_map.64 = bf16[512,1024]{1,0:T(8,128)(2,1)S(1)} custom-call(bf16[512,1024]{1,0:T(8,128)(2,1)} %tokens_hbm.1, bf16[1024,1024]{1,0:T(8,128)(2,1)} %value_hbm.1, bf16[1024,1024]{1,0:T(8,128)(2,1)} %gate_hbm.1, bf16[16,2,32,1024]{3,2,1,0:T(8,128)(2,1)} %bitcast.3, bf16[16,1024]{1,0:T(8,128)(2,1)} %bitcast.4, f32[1,16]{1,0:T(1,128)} %bitcast.5), custom_call_target="tpu_custom_call" | custom-call | tf_op jit(solution)/shard_map/pallas_call | solution.py:368
  51.3 1.0 %copy.8 = bf16[512,1024]{1,0:T(8,128)(2,1)} copy(bf16[512,1024]{1,0:T(8,128)(2,1)S(1)} %shard_map.64) | data formatting | bytes 2097152
